TPU v7x, 256 devices: a whole 4x4x8 slice. The times are simulated.
256 devices in a mesh: seq: 32 (over x, z), head: 8 (over y, core).
Axes of the slice: x: 4, y: 4, z: 8, core: 2. Of those that a mesh axis runs over, the one named last changes fastest.
Arguments:
- tokens: bfloat16 [16384, 4096], P('seq'), may hold values from -6 to 6
- w_xz: bfloat16 [4096, 2, 4096], P('seq', None, 'head'), may hold values from -0.09375 to 0.09375
- w_bc: bfloat16 [4096, 256], P('seq'), may hold values from -0.09375 to 0.09375
- conv_x: float32 [4, 4096], P(None, 'head'), may hold values from -3 to 3
- conv_bc: float32 [4, 256], replicated, may hold values from -3 to 3
- tail_x: bfloat16 [3, 4096], P(None, 'head'), may hold values from -6 to 6
- tail_bc: bfloat16 [3, 256], replicated, may hold values from -6 to 6
- decay_code: int32 [16384, 64], P('seq', 'head'), may hold values from 0 to 196608, as said below
- skip_gain: float32 [64], P('head'), may hold values from 0.5 to 2
- state_in: float32 [64, 64, 128], P('head'), may hold values from -180 to 180
- norm_gain: float32 [4096], P('head'), may hold values from 0.1 to 1.9
- w_out: bfloat16 [4096, 4096], P('head', 'seq'), may hold values from -0.1875 to 0.1875
Outputs:
- mixed: bfloat16 [16384, 4096], P('seq', 'head')
Inputs may be any that keep to these rules, and one draw needn't show every extreme that they name: `decay_code`: the decay factor of a token and head is exp(-code / 262144).
All inputs are finite; a program needn't handle non-finite values.
Results may differ from a plain program's by a relative error of at most 0.0085.
Values may be sent and summed in bfloat16 or wider, within the bound.
A program may use at most 128 MiB of HBM per device.

v0:
```python
import jax
import jax.numpy as jnp
from jax import lax
from jax.sharding import PartitionSpec as P

Q = 256


def passed_along(value, axis, by):
    size = lax.axis_size(axis)
    pairs = [(i, i + by) for i in range(size) if 0 <= i + by < size]
    return lax.ppermute(value, axis, pairs)


def depthwise(pre, tail, kernel):
    whole = jnp.concatenate([tail, pre], axis=0).astype(jnp.float32)
    length = pre.shape[0]
    total = jnp.zeros((length, pre.shape[1]), jnp.float32)
    for offset in range(kernel.shape[0]):
        total = total + kernel[offset] * whole[offset : offset + length]
    return jax.nn.silu(total).astype(jnp.bfloat16)


def block_step(state, inputs):
    xval, bval, cval, logdec = inputs
    cum = jnp.cumsum(logdec, axis=0)
    span = cum.shape[0]
    places = jnp.arange(span)
    lower = places[:, None] >= places[None, :]
    cumt = cum.T
    diff = cumt[:, :, None] - cumt[:, None, :]
    decay = jnp.where(lower[None], jnp.exp(jnp.where(lower[None], diff, 0.0)), 0.0)
    scores = jnp.dot(cval, bval.T, preferred_element_type=jnp.float32)
    weights = (decay * scores[None]).astype(jnp.bfloat16)
    inner = jnp.einsum("hts,shp->thp", weights, xval, preferred_element_type=jnp.float32)
    carried = jnp.einsum(
        "tn,hpn->thp", cval.astype(jnp.float32), state, precision=lax.Precision.HIGHEST
    )
    carried = carried * jnp.exp(cum)[:, :, None]
    tail_decay = jnp.exp(cum[-1][None, :] - cum)
    decayed_b = (tail_decay.T[:, :, None] * bval.astype(jnp.float32)[None]).astype(jnp.bfloat16)
    added = jnp.einsum("hsn,shp->hpn", decayed_b, xval, preferred_element_type=jnp.float32)
    new_state = jnp.exp(cum[-1])[:, None, None] * state + added
    return (new_state, inner + carried)


def local(
    tokens,
    w_xz,
    w_bc,
    conv_x,
    conv_bc,
    tail_x,
    tail_bc,
    decay_code,
    skip_gain,
    state_in,
    norm_gain,
    w_out,
):
    rows = tokens.shape[0]
    heads, head_dim, nstate = state_in.shape
    inner = heads * head_dim
    seq_count = lax.axis_size("seq")
    first = lax.axis_index("seq") == 0
    pieces = (
        lax.all_gather(w_xz, "seq", axis=0, tiled=True),
        lax.all_gather(w_bc, "seq", axis=0, tiled=True),
    )
    count = pieces[0].shape[0]
    xz = jnp.dot(tokens, pieces[0].reshape(count, 2 * inner), preferred_element_type=jnp.float32)
    bc_sum = jnp.dot(tokens, pieces[1], preferred_element_type=jnp.float32)
    x_pre = xz[:, :inner].astype(jnp.bfloat16)
    z_val = xz[:, inner:].astype(jnp.bfloat16)
    bc_pre = bc_sum.astype(jnp.bfloat16)
    lag = conv_x.shape[0] - 1
    before_x, before_bc = passed_along((x_pre[rows - lag :], bc_pre[rows - lag :]), "seq", 1)
    before_x = jnp.where(first, tail_x, before_x)
    before_bc = jnp.where(first, tail_bc, before_bc)
    x_conv = depthwise(x_pre, before_x, conv_x)
    bc_conv = depthwise(bc_pre, before_bc, conv_bc)
    b_val = bc_conv[:, :nstate]
    c_val = bc_conv[:, nstate:]
    logdec = -decay_code.astype(jnp.float32) / (16.0 * rows * seq_count)
    blocks = rows // Q
    inputs = (
        x_conv.reshape(blocks, Q, heads, head_dim),
        b_val.reshape(blocks, Q, nstate),
        c_val.reshape(blocks, Q, nstate),
        logdec.reshape(blocks, Q, heads),
    )
    local_state, parts = lax.scan(block_step, jnp.zeros_like(state_in), inputs)
    parts = parts.reshape(rows, heads, head_dim)
    cum_range = jnp.cumsum(logdec, axis=0)
    range_decay = jnp.exp(cum_range[-1])

    def link(step, incoming):
        outgoing = range_decay[:, None, None] * incoming + local_state
        received = passed_along(outgoing, "seq", 1)
        return jnp.where(first, state_in, received)

    opening = jnp.where(first, state_in, jnp.zeros_like(state_in))
    incoming = lax.fori_loop(0, seq_count - 1, link, opening)
    correction = jnp.einsum(
        "tn,hpn->thp", c_val.astype(jnp.float32), incoming, precision=lax.Precision.HIGHEST
    )
    parts = (parts + correction * jnp.exp(cum_range)[:, :, None]).reshape(rows, inner)
    y_val = parts / nstate + jnp.repeat(skip_gain, head_dim)[None, :] * x_conv.astype(jnp.float32)
    gated = y_val * jax.nn.silu(z_val.astype(jnp.float32))
    total_sq = lax.psum(jnp.sum(gated * gated, axis=1), "head")
    meansq = total_sq / (inner * lax.axis_size("head"))
    normed = (gated * lax.rsqrt(meansq[:, None] + 1e-05) * norm_gain[None, :]).astype(jnp.bfloat16)
    partial_out = jnp.dot(
        normed, lax.all_gather(w_out, "seq", axis=1, tiled=True), preferred_element_type=jnp.float32
    )
    result = lax.psum_scatter(partial_out, "head", scatter_dimension=1, tiled=True)
    return result.astype(jnp.bfloat16)


def solution(mesh):
    return jax.shard_map(
        local,
        mesh=mesh,
        in_specs=(
            P("seq", None),
            P("seq", None, "head"),
            P("seq", None),
            P(None, "head"),
            P(),
            P(None, "head"),
            P(),
            P("seq", "head"),
            P("head"),
            P("head", None, None),
            P("head"),
            P("head", "seq"),
        ),
        out_specs=P("seq", "head"),
        check_vma=False,
    )
```

profile of v0, /device:TPU:1, one launch (start us, length us, event | category | flops | bytes accessed | tf_op | source)
XLA Modules:
  0.0 687.8 jit_solution(6303912154717134488)
XLA Ops:
  13.6 74.2 %all-gather.6.cloned.1.call-done = bf16[4096,256]{1,0:T(8,128)(2,1)} async-done(((bf16[128,256]{1,0:T(8,128)(2,1)}), bf16[4096,256]{1,0:T(8,128)(2,1)}) %all-gather.6.cloned.1.call-update) | async-done | bytes 2097168 | tf_op jit(solution)/shard_map/all_gather | solution.py:68
  95.5 93.9 %all-gather.4.cloned.1.call-done = bf16[4096,2,512]{2,1,0:T(2,128)(2,1)} async-done(((bf16[128,2,512]{2,1,0:T(2,128)(2,1)}), bf16[4096,2,512]{2,1,0:T(2,128)(2,1)}) %all-gather.4.cloned.1.call-update) | async-done | bytes 8388624 | tf_op jit(solution)/shard_map/all_gather | solution.py:67
  189.4 9.3 %copy.40 = bf16[512,8,2,512]{3,1,2,0:T(8,128)(2,1)} copy(bf16[512,8,2,512]{3,2,1,0:T(2,128)(2,1)} %bitcast.88) | data formatting | bytes 16777216
  198.7 9.3 %convolution_convert_fusion = bf16[512,1024]{1,0:T(8,128)(2,1)S(1)} fusion(bf16[512,4096]{1,0:T(8,128)(2,1)} %param.16, bf16[4096,1024]{1,0:T(8,128)(2,1)} %bitcast.89), kind=kOutput, calls=%fused_computation.44 | convolution fusion | flops 4295491584 | bytes 13631488 | tf_op jit(solution)/shard_map/dot_general | solution.py:71
  212.1 30.3 %while.24 = (s32[]{:T(128)}, f32[8,64,128]{2,1,0:T(8,128)S(1)}, f32[2,256,8,64]{1,0,3,2:T(2,128)}, f32[2,256,8]{1,2,0:T(8,128)S(1)}, bf16[2,256,8,64]{1,3,2,0:T(...) while((s32[]{:T(128)}, f32[8,64,128]{2,1,0:T(8,128)S(1)}, ...), condition=%wide.region_3.4_spmd.clone, body=%wide.region_0.3_spmd.clone.sunk | while | flops 322801696 | bytes 6277456 | solution.py:92
  215.2 11.5 %dynamic_update_slice.6 = f32[2,256,8,64]{1,0,3,2:T(2,128)} dynamic-update-slice(f32[2,256,8,64]{1,0,3,2:T(2,128)} %get-tuple-element.276, f32[1,256,8,64]{1,0,3,2:T(1,128)S(1)} %copy.42, s32[]{:T(128)} %get-tuple-element.274, s32[]{:T(128)} %constant.46.clone.1..sunk, s32[]{:T(128)} %constant.46.clone.1..sunk, s32[]{:T(128)} %constant.46.clone.1..sunk) | dynamic-update-slice | bytes 1048580 | tf_op jit(solution)/shard_map/while/body/jit(dynamic_update_index_in_dim)/dynamic_update_slice | solution.py:92
  230.3 11.5 %dynamic_update_slice.6 = f32[2,256,8,64]{1,0,3,2:T(2,128)} dynamic-update-slice(f32[2,256,8,64]{1,0,3,2:T(2,128)} %get-tuple-element.276, f32[1,256,8,64]{1,0,3,2:T(1,128)S(1)} %copy.42, s32[]{:T(128)} %get-tuple-element.274, s32[]{:T(128)} %constant.46.clone.1..sunk, s32[]{:T(128)} %constant.46.clone.1..sunk, s32[]{:T(128)} %constant.46.clone.1..sunk) | dynamic-update-slice | bytes 1048580 | tf_op jit(solution)/shard_map/while/body/jit(dynamic_update_index_in_dim)/dynamic_update_slice | solution.py:92
  244.6 299.9 %while.23 = (s32[]{:T(128)}, f32[8,64,128]{2,1,0:T(8,128)S(1)}, pred[]{:T(512)}, f32[8]{0:T(128)S(1)}, f32[8,64,128]{2,1,0:T(8,128)S(1)}, /*index=5*/f32[8,64,128]{2,1,0:T(8,128)S(1)}, s32[]{:T(128)}) while((s32[]{:T(128)}, f32[8,64,128]{2,1,0:T(8,128)S(1)}, pred[]{:T(512)}, f32[8]{0:T(128)S(1)}, f32[8,64,128]{2,1,0:T(8,128)S(1)}, ...), condition=%wide.region_7.8_spmd, body=%wide.region_6.7_spmd.sunk | while | flops 196610 | bytes 2621590 | solution.py:103
  248.6 8.4 %collective-permute-done = f32[8,64,128]{2,1,0:T(8,128)S(1)} collective-permute-done((f32[8,64,128]{2,1,0:T(8,128)S(1)}, f32[8,64,128]{2,1,0:T(8,128)S(1)}, u32[]{:S(2)}, u32[]{:S(2)}) %collective-permute-start) | collective-permute-done | bytes 262176 | tf_op jit(solution)/shard_map/while/body/eval_jaxpr/ppermute | solution.py:12
  261.3 7.3 %collective-permute-done = f32[8,64,128]{2,1,0:T(8,128)S(1)} collective-permute-done((f32[8,64,128]{2,1,0:T(8,128)S(1)}, f32[8,64,128]{2,1,0:T(8,128)S(1)}, u32[]{:S(2)}, u32[]{:S(2)}) %collective-permute-start) | collective-permute-done | bytes 262176 | tf_op jit(solution)/shard_map/while/body/eval_jaxpr/ppermute | solution.py:12
  314.4 5.8 collective-permute-done
  337.7 6.9 %collective-permute-start = (f32[8,64,128]{2,1,0:T(8,128)S(1)}, f32[8,64,128]{2,1,0:T(8,128)S(1)}, u32[]{:S(2)}, u32[]{:S(2)}) collective-permute-start(f32[8,64,128]{2,1,0:T(8,128)S(1)} %multiply_add_fusion.2), channel_id=1, source_target_pairs={{0,8},{8,16},{16,24},{24,32},{32,40},{40,48},{48,56},{56,64},{64,7... | collective-permute-start | bytes 786440 | tf_op jit(solution)/shard_map/while/body/eval_jaxpr/ppermute | solution.py:12
  411.9 5.9 collective-permute-start
  417.8 5.8 collective-permute-done
  459.3 10.4 %collective-permute-start = (f32[8,64,128]{2,1,0:T(8,128)S(1)}, f32[8,64,128]{2,1,0:T(8,128)S(1)}, u32[]{:S(2)}, u32[]{:S(2)}) collective-permute-start(f32[8,64,128]{2,1,0:T(8,128)S(1)} %multiply_add_fusion.2), channel_id=1, source_target_pairs={{0,8},{8,16},{16,24},{24,32},{32,40},{40,48},{48,56},{56,64},{64,7... | collective-permute-start | bytes 786440 | tf_op jit(solution)/shard_map/while/body/eval_jaxpr/ppermute | solution.py:12
  473.2 5.7 collective-permute-start
  499.8 6.2 collective-permute-start
  509.7 6.2 collective-permute-start
  520.3 6.1 collective-permute-start
  531.5 6.9 collective-permute-start
  538.4 6.1 collective-permute-done
  552.1 45.7 %psum.7 = f32[512]{0:T(512)S(1)} all-reduce(f32[512]{0:T(512)S(1)} %get-tuple-element.160), channel_id=1, replica_groups=mesh['seq'=32,'head'=8] {'head'}, use_global_device_ids=true, to_apply=%region_9.10 | all-reduce | flops 512 | bytes 4096 | tf_op jit(solution)/shard_map/psum | solution.py:110
  597.8 7.8 %fusion.38 = f32[512,4096]{1,0:T(8,128)} fusion(bf16[512,4096]{1,0:T(8,128)(2,1)} %all-gather.8.cloned.1.call-done, f32[512,512]{1,0:T(8,128)S(1)} %get-tuple-element.161, f32[512]{0:T(512)S(1)} %copy-done.3, f32[512]{0:T(512)S(1)} %add_rsqrt_fusion), kind=kOutput, calls=%fused_computation.66 | convolution fusion | flops 2148270080 | bytes 13635584 | tf_op jit(solution)/shard_map/dot_general | solution.py:113
  605.6 73.5 %reduce-scatter.2.cloned.1.call-done = f32[512,512]{1,0:T(8,128)} async-done(((f32[512,4096]{1,0:T(8,128)}), f32[512,512]{1,0:T(8,128)}) %reduce-scatter.2.cloned.1.call-update) | async-done | bytes 1048592 | tf_op jit(solution)/shard_map/reduce_scatter | solution.py:116
  (203 shorter events, 248.8 us)
Async XLA Ops:
  6.5 81.3 %all-gather.6.cloned.1.call-start = ((), (), s32[]{:S(2)}) async-start(), calls=%async_computation.2 | async-start | bytes 2162688 | tf_op jit(solution)/shard_map/all_gather | solution.py:68
  7.3 182.2 %all-gather.4.cloned.1.call-start = ((), (), s32[]{:S(2)}) async-start(), calls=%async_computation.1 | async-start | bytes 8650752 | tf_op jit(solution)/shard_map/all_gather | solution.py:67
  8.0 589.8 %all-gather.8.cloned.1.call-start = ((), (), s32[]{:S(2)}) async-start(), calls=%async_computation.3 | async-start | bytes 4325376 | tf_op jit(solution)/shard_map/all_gather | solution.py:114
  8.7 670.4 %reduce-scatter.2.cloned.1.call-start = ((), (), s32[]{:S(2)}) async-start(), calls=%async_computation.4 | async-start | bytes 9437184 | tf_op jit(solution)/shard_map/reduce_scatter | solution.py:116
  244.7 12.3 %collective-permute-start = (f32[8,64,128]{2,1,0:T(8,128)S(1)}, f32[8,64,128]{2,1,0:T(8,128)S(1)}, u32[]{:S(2)}, u32[]{:S(2)}) collective-permute-start(f32[8,64,128]{2,1,0:T(8,128)S(1)} %multiply_add_fusion.2), channel_id=1, source_target_pairs={{0,8},{8,16},{16,24},{24,32},{32,40},{40,48},{48,56},{56,64},{64,7... | collective-permute-start | bytes 786440 | tf_op jit(solution)/shard_map/while/body/eval_jaxpr/ppermute | solution.py:12
  257.1 11.6 %collective-permute-start = (f32[8,64,128]{2,1,0:T(8,128)S(1)}, f32[8,64,128]{2,1,0:T(8,128)S(1)}, u32[]{:S(2)}, u32[]{:S(2)}) collective-permute-start(f32[8,64,128]{2,1,0:T(8,128)S(1)} %multiply_add_fusion.2), channel_id=1, source_target_pairs={{0,8},{8,16},{16,24},{24,32},{32,40},{40,48},{48,56},{56,64},{64,7... | collective-permute-start | bytes 786440 | tf_op jit(solution)/shard_map/while/body/eval_jaxpr/ppermute | solution.py:12
  268.8 9.0 %collective-permute-start = (f32[8,64,128]{2,1,0:T(8,128)S(1)}, f32[8,64,128]{2,1,0:T(8,128)S(1)}, u32[]{:S(2)}, u32[]{:S(2)}) collective-permute-start(f32[8,64,128]{2,1,0:T(8,128)S(1)} %multiply_add_fusion.2), channel_id=1, source_target_pairs={{0,8},{8,16},{16,24},{24,32},{32,40},{40,48},{48,56},{56,64},{64,7... | collective-permute-start | bytes 786440 | tf_op jit(solution)/shard_map/while/body/eval_jaxpr/ppermute | solution.py:12
  301.3 9.1 %collective-permute-start = (f32[8,64,128]{2,1,0:T(8,128)S(1)}, f32[8,64,128]{2,1,0:T(8,128)S(1)}, u32[]{:S(2)}, u32[]{:S(2)}) collective-permute-start(f32[8,64,128]{2,1,0:T(8,128)S(1)} %multiply_add_fusion.2), channel_id=1, source_target_pairs={{0,8},{8,16},{16,24},{24,32},{32,40},{40,48},{48,56},{56,64},{64,7... | collective-permute-start | bytes 786440 | tf_op jit(solution)/shard_map/while/body/eval_jaxpr/ppermute | solution.py:12
  310.5 9.6 %collective-permute-start = (f32[8,64,128]{2,1,0:T(8,128)S(1)}, f32[8,64,128]{2,1,0:T(8,128)S(1)}, u32[]{:S(2)}, u32[]{:S(2)}) collective-permute-start(f32[8,64,128]{2,1,0:T(8,128)S(1)} %multiply_add_fusion.2), channel_id=1, source_target_pairs={{0,8},{8,16},{16,24},{24,32},{32,40},{40,48},{48,56},{56,64},{64,7... | collective-permute-start | bytes 786440 | tf_op jit(solution)/shard_map/while/body/eval_jaxpr/ppermute | solution.py:12
  320.3 9.0 %collective-permute-start = (f32[8,64,128]{2,1,0:T(8,128)S(1)}, f32[8,64,128]{2,1,0:T(8,128)S(1)}, u32[]{:S(2)}, u32[]{:S(2)}) collective-permute-start(f32[8,64,128]{2,1,0:T(8,128)S(1)} %multiply_add_fusion.2), channel_id=1, source_target_pairs={{0,8},{8,16},{16,24},{24,32},{32,40},{40,48},{48,56},{56,64},{64,7... | collective-permute-start | bytes 786440 | tf_op jit(solution)/shard_map/while/body/eval_jaxpr/ppermute | solution.py:12
  337.7 11.4 %collective-permute-start = (f32[8,64,128]{2,1,0:T(8,128)S(1)}, f32[8,64,128]{2,1,0:T(8,128)S(1)}, u32[]{:S(2)}, u32[]{:S(2)}) collective-permute-start(f32[8,64,128]{2,1,0:T(8,128)S(1)} %multiply_add_fusion.2), channel_id=1, source_target_pairs={{0,8},{8,16},{16,24},{24,32},{32,40},{40,48},{48,56},{56,64},{64,7... | collective-permute-start | bytes 786440 | tf_op jit(solution)/shard_map/while/body/eval_jaxpr/ppermute | solution.py:12
  374.2 8.6 %collective-permute-start = (f32[8,64,128]{2,1,0:T(8,128)S(1)}, f32[8,64,128]{2,1,0:T(8,128)S(1)}, u32[]{:S(2)}, u32[]{:S(2)}) collective-permute-start(f32[8,64,128]{2,1,0:T(8,128)S(1)} %multiply_add_fusion.2), channel_id=1, source_target_pairs={{0,8},{8,16},{16,24},{24,32},{32,40},{40,48},{48,56},{56,64},{64,7... | collective-permute-start | bytes 786440 | tf_op jit(solution)/shard_map/while/body/eval_jaxpr/ppermute | solution.py:12
  391.5 9.3 %collective-permute-start = (f32[8,64,128]{2,1,0:T(8,128)S(1)}, f32[8,64,128]{2,1,0:T(8,128)S(1)}, u32[]{:S(2)}, u32[]{:S(2)}) collective-permute-start(f32[8,64,128]{2,1,0:T(8,128)S(1)} %multiply_add_fusion.2), channel_id=1, source_target_pairs={{0,8},{8,16},{16,24},{24,32},{32,40},{40,48},{48,56},{56,64},{64,7... | collective-permute-start | bytes 786440 | tf_op jit(solution)/shard_map/while/body/eval_jaxpr/ppermute | solution.py:12
  400.9 10.9 %collective-permute-start = (f32[8,64,128]{2,1,0:T(8,128)S(1)}, f32[8,64,128]{2,1,0:T(8,128)S(1)}, u32[]{:S(2)}, u32[]{:S(2)}) collective-permute-start(f32[8,64,128]{2,1,0:T(8,128)S(1)} %multiply_add_fusion.2), channel_id=1, source_target_pairs={{0,8},{8,16},{16,24},{24,32},{32,40},{40,48},{48,56},{56,64},{64,7... | collective-permute-start | bytes 786440 | tf_op jit(solution)/shard_map/while/body/eval_jaxpr/ppermute | solution.py:12
  411.9 11.8 %collective-permute-start = (f32[8,64,128]{2,1,0:T(8,128)S(1)}, f32[8,64,128]{2,1,0:T(8,128)S(1)}, u32[]{:S(2)}, u32[]{:S(2)}) collective-permute-start(f32[8,64,128]{2,1,0:T(8,128)S(1)} %multiply_add_fusion.2), channel_id=1, source_target_pairs={{0,8},{8,16},{16,24},{24,32},{32,40},{40,48},{48,56},{56,64},{64,7... | collective-permute-start | bytes 786440 | tf_op jit(solution)/shard_map/while/body/eval_jaxpr/ppermute | solution.py:12
  423.8 10.4 %collective-permute-start = (f32[8,64,128]{2,1,0:T(8,128)S(1)}, f32[8,64,128]{2,1,0:T(8,128)S(1)}, u32[]{:S(2)}, u32[]{:S(2)}) collective-permute-start(f32[8,64,128]{2,1,0:T(8,128)S(1)} %multiply_add_fusion.2), channel_id=1, source_target_pairs={{0,8},{8,16},{16,24},{24,32},{32,40},{40,48},{48,56},{56,64},{64,7... | collective-permute-start | bytes 786440 | tf_op jit(solution)/shard_map/while/body/eval_jaxpr/ppermute | solution.py:12
  434.4 8.7 %collective-permute-start = (f32[8,64,128]{2,1,0:T(8,128)S(1)}, f32[8,64,128]{2,1,0:T(8,128)S(1)}, u32[]{:S(2)}, u32[]{:S(2)}) collective-permute-start(f32[8,64,128]{2,1,0:T(8,128)S(1)} %multiply_add_fusion.2), channel_id=1, source_target_pairs={{0,8},{8,16},{16,24},{24,32},{32,40},{40,48},{48,56},{56,64},{64,7... | collective-permute-start | bytes 786440 | tf_op jit(solution)/shard_map/while/body/eval_jaxpr/ppermute | solution.py:12
  459.3 13.7 %collective-permute-start = (f32[8,64,128]{2,1,0:T(8,128)S(1)}, f32[8,64,128]{2,1,0:T(8,128)S(1)}, u32[]{:S(2)}, u32[]{:S(2)}) collective-permute-start(f32[8,64,128]{2,1,0:T(8,128)S(1)} %multiply_add_fusion.2), channel_id=1, source_target_pairs={{0,8},{8,16},{16,24},{24,32},{32,40},{40,48},{48,56},{56,64},{64,7... | collective-permute-start | bytes 786440 | tf_op jit(solution)/shard_map/while/body/eval_jaxpr/ppermute | solution.py:12
  473.2 9.0 %collective-permute-start = (f32[8,64,128]{2,1,0:T(8,128)S(1)}, f32[8,64,128]{2,1,0:T(8,128)S(1)}, u32[]{:S(2)}, u32[]{:S(2)}) collective-permute-start(f32[8,64,128]{2,1,0:T(8,128)S(1)} %multiply_add_fusion.2), channel_id=1, source_target_pairs={{0,8},{8,16},{16,24},{24,32},{32,40},{40,48},{48,56},{56,64},{64,7... | collective-permute-start | bytes 786440 | tf_op jit(solution)/shard_map/while/body/eval_jaxpr/ppermute | solution.py:12
  482.3 8.7 %collective-permute-start = (f32[8,64,128]{2,1,0:T(8,128)S(1)}, f32[8,64,128]{2,1,0:T(8,128)S(1)}, u32[]{:S(2)}, u32[]{:S(2)}) collective-permute-start(f32[8,64,128]{2,1,0:T(8,128)S(1)} %multiply_add_fusion.2), channel_id=1, source_target_pairs={{0,8},{8,16},{16,24},{24,32},{32,40},{40,48},{48,56},{56,64},{64,7... | collective-permute-start | bytes 786440 | tf_op jit(solution)/shard_map/while/body/eval_jaxpr/ppermute | solution.py:12
  499.8 9.7 %collective-permute-start = (f32[8,64,128]{2,1,0:T(8,128)S(1)}, f32[8,64,128]{2,1,0:T(8,128)S(1)}, u32[]{:S(2)}, u32[]{:S(2)}) collective-permute-start(f32[8,64,128]{2,1,0:T(8,128)S(1)} %multiply_add_fusion.2), channel_id=1, source_target_pairs={{0,8},{8,16},{16,24},{24,32},{32,40},{40,48},{48,56},{56,64},{64,7... | collective-permute-start | bytes 786440 | tf_op jit(solution)/shard_map/while/body/eval_jaxpr/ppermute | solution.py:12
  509.7 10.5 %collective-permute-start = (f32[8,64,128]{2,1,0:T(8,128)S(1)}, f32[8,64,128]{2,1,0:T(8,128)S(1)}, u32[]{:S(2)}, u32[]{:S(2)}) collective-permute-start(f32[8,64,128]{2,1,0:T(8,128)S(1)} %multiply_add_fusion.2), channel_id=1, source_target_pairs={{0,8},{8,16},{16,24},{24,32},{32,40},{40,48},{48,56},{56,64},{64,7... | collective-permute-start | bytes 786440 | tf_op jit(solution)/shard_map/while/body/eval_jaxpr/ppermute | solution.py:12
  520.3 11.0 %collective-permute-start = (f32[8,64,128]{2,1,0:T(8,128)S(1)}, f32[8,64,128]{2,1,0:T(8,128)S(1)}, u32[]{:S(2)}, u32[]{:S(2)}) collective-permute-start(f32[8,64,128]{2,1,0:T(8,128)S(1)} %multiply_add_fusion.2), channel_id=1, source_target_pairs={{0,8},{8,16},{16,24},{24,32},{32,40},{40,48},{48,56},{56,64},{64,7... | collective-permute-start | bytes 786440 | tf_op jit(solution)/shard_map/while/body/eval_jaxpr/ppermute | solution.py:12
  531.5 12.9 %collective-permute-start = (f32[8,64,128]{2,1,0:T(8,128)S(1)}, f32[8,64,128]{2,1,0:T(8,128)S(1)}, u32[]{:S(2)}, u32[]{:S(2)}) collective-permute-start(f32[8,64,128]{2,1,0:T(8,128)S(1)} %multiply_add_fusion.2), channel_id=1, source_target_pairs={{0,8},{8,16},{16,24},{24,32},{32,40},{40,48},{48,56},{56,64},{64,7... | collective-permute-start | bytes 786440 | tf_op jit(solution)/shard_map/while/body/eval_jaxpr/ppermute | solution.py:12
  (20 other events, 433.9 us)
Sparse Core Ops, SparseCore 0:
  9.9 77.8 all-gather.5
  90.4 98.9 all-gather.3
  191.9 85.3 all-gather.7
  605.7 73.3 reduce-scatter.1
where the time goes:
time: 691 us; the launch traced here: 688 us
  waiting for transfers between devices  379 us (55%)
  starting transfers between devices  164 us (24%)
  blocking collectives  45.7 us (7%)
  local copies, waits for them, and re-layouts  42.3 us (6%)
  matrix products  27.4 us (4%)
  other arithmetic  14.1 us (2%)
  between operations  13.4 us (2%)
    ppermute x33, starting transfers between devices, passed_along(): return lax.ppermute(value, axis, pairs)  164 us
    ppermute x33, waiting for transfers between devices, passed_along(): return lax.ppermute(value, axis, pairs)  136 us
    all_gather x1, waiting for transfers between devices, local(): lax.all_gather(w_xz, 'seq', axis=0, tiled=True)  93.9 us
    all_gather x1, waiting for transfers between devices, local(): lax.all_gather(w_bc, 'seq', axis=0, tiled=True)  74.2 us
    reduce_scatter x1, waiting for transfers between devices, local(): lax.psum_scatter(partial_out, 'head', scatter_dimension=1, tiled=True)  73.5 us
    psum x1, blocking collectives, local(): total_sq = lax.psum(jnp.sum(gated * gated, axis=1), 'head')  45.7 us
    dynamic_update_slice x4, local copies, waits for them, and re-layouts, local(): local_state, parts = lax.scan(block_step, jnp.zeros_like(state_in), inputs)  24.1 us
  transfers between devices with their start and end apart: 37, of which 36 were waited for; matrix products, arithmetic and copies ran while one was open for 11% of the time, Pallas kernels for 0%

commit v1 on v0

--- a/solution.py
+++ b/solution.py
@@ -4,6 +4,15 @@
 from jax.sharding import PartitionSpec as P
 
 Q = 256
+
+
+def view_weights_on(w_in, k_dim, link_axis):
+    devs = lax.axis_size(link_axis)
+    n_now = range(w_in.ndim)
+    res = map(lambda p: devs if p == k_dim else 1, n_now)
+    stack_in = list(res)
+    heard = jnp.tile(w_in, stack_in)
+    return lax.all_to_all(heard, link_axis, split_axis=k_dim, concat_axis=k_dim, tiled=True)
 
 
 def passed_along(value, axis, by):
@@ -63,10 +72,7 @@
     inner = heads * head_dim
     seq_count = lax.axis_size("seq")
     first = lax.axis_index("seq") == 0
-    pieces = (
-        lax.all_gather(w_xz, "seq", axis=0, tiled=True),
-        lax.all_gather(w_bc, "seq", axis=0, tiled=True),
-    )
+    pieces = (lax.all_gather(w_xz, "seq", axis=0, tiled=True), view_weights_on(w_bc, 0, "seq"))
     count = pieces[0].shape[0]
     xz = jnp.dot(tokens, pieces[0].reshape(count, 2 * inner), preferred_element_type=jnp.float32)
     bc_sum = jnp.dot(tokens, pieces[1], preferred_element_type=jnp.float32)

time: 691 us -> 634 us (0.918)
  waiting for transfers between devices: 379 us -> 304 us
  starting transfers between devices: 164 us -> 182 us
    all_gather x1 -> x0, waiting for transfers between devices: 74.2 us -> none  [local(): lax.all_gather(w_bc, 'seq', axis=0, tiled=True)]
    all_to_all x0 -> x1, waiting for transfers between devices: none -> 56.6 us  [view_weights_on(): lax.all_to_all(heard, link_axis, split_axis=k_dim, concat_axis=k_dim, til...]
    all_gather x1, waiting for transfers between devices: 93.9 us -> 40.1 us  [local(): lax.all_gather(w_xz, 'seq', axis=0, tiled=True)]
    all_to_all x0 -> x1, starting transfers between devices: none -> 12 us  [view_weights_on(): lax.all_to_all(heard, link_axis, split_axis=k_dim, concat_axis=k_dim, til...]
  transfers between devices with their start and end apart: 37 -> 37, of which waited for: 36 -> 36; matrix products, arithmetic and copies ran while one was open for 11% -> 12% of each run, Pallas kernels for 0% -> 0%
where the time goes in v1:
time: 634 us; the launch traced here: 632 us
  waiting for transfers between devices  304 us (48%)
  starting transfers between devices  182 us (29%)
  blocking collectives  45.8 us (7%)
  local copies, waits for them, and re-layouts  45.2 us (7%)
  matrix products  26.9 us (4%)
  between operations  13.4 us (2%)
  other arithmetic  12.5 us (2%)
    ppermute x33, starting transfers between devices, passed_along(): return lax.ppermute(value, axis, pairs)  170 us
    ppermute x33, waiting for transfers between devices, passed_along(): return lax.ppermute(value, axis, pairs)  130 us
    reduce_scatter x1, waiting for transfers between devices, local(): lax.psum_scatter(partial_out, 'head', scatter_dimension=1, tiled=True)  76.3 us
    all_to_all x1, waiting for transfers between devices, view_weights_on(): lax.all_to_all(heard, link_axis, split_axis=k_dim, concat_axis=k_dim, til...  56.6 us
    psum x1, blocking collectives, local(): total_sq = lax.psum(jnp.sum(gated * gated, axis=1), 'head')  45.8 us
    all_gather x1, waiting for transfers between devices, local(): lax.all_gather(w_xz, 'seq', axis=0, tiled=True)  40.1 us
    dynamic_update_slice x4, local copies, waits for them, and re-layouts, local(): local_state, parts = lax.scan(block_step, jnp.zeros_like(state_in), inputs)  24.1 us
  transfers between devices with their start and end apart: 37, of which 36 were waited for; matrix products, arithmetic and copies ran while one was open for 12% of the time, Pallas kernels for 0%

profile of v1, /device:TPU:1, one launch (start us, length us, event | category | flops | bytes accessed | tf_op | source)
XLA Modules:
  0.0 631.5 jit_solution(11345245610435511484)
XLA Ops:
  9.7 12.0 %all-to-all-start = ((bf16[32,128,256]{2,1,0:T(8,128)(2,1)}), bf16[32,128,256]{2,1,0:T(8,128)(2,1)S(1)}, u32[]{:S(2)}, u32[]{:S(2)}) async-start(bf16[32,128,256]{2,1,0:T(8,128)(2,1)} %tile.2), calls=%async_computation | async-start | bytes 4194304 | tf_op jit(solution)/shard_map/all_to_all | solution.py:15
  24.1 56.6 %all-to-all-done = bf16[32,128,256]{2,1,0:T(8,128)(2,1)S(1)} async-done(((bf16[32,128,256]{2,1,0:T(8,128)(2,1)}), bf16[32,128,256]{2,1,0:T(8,128)(2,1)S(1)}, u32[]{:S(2)}, u32[]{:S(2)}) %all-to-all-start) | async-done | bytes 2097184 | tf_op jit(solution)/shard_map/all_to_all | solution.py:15
  89.5 40.1 %all-gather.3.cloned.1.call-done = bf16[4096,2,512]{2,1,0:T(2,128)(2,1)} async-done(((bf16[128,2,512]{2,1,0:T(2,128)(2,1)}), bf16[4096,2,512]{2,1,0:T(2,128)(2,1)}) %all-gather.3.cloned.1.call-update) | async-done | bytes 8388624 | tf_op jit(solution)/shard_map/all_gather | solution.py:75
  129.6 9.3 %copy.40 = bf16[512,8,2,512]{3,1,2,0:T(8,128)(2,1)} copy(bf16[512,8,2,512]{3,2,1,0:T(2,128)(2,1)} %bitcast.89) | data formatting | bytes 16777216
  138.9 9.3 %convolution_convert_fusion = bf16[512,1024]{1,0:T(8,128)(2,1)S(1)} fusion(bf16[512,4096]{1,0:T(8,128)(2,1)} %param.16, bf16[4096,1024]{1,0:T(8,128)(2,1)} %bitcast.90), kind=kOutput, calls=%fused_computation.44 | convolution fusion | flops 4295491584 | bytes 13631488 | tf_op jit(solution)/shard_map/dot_general | solution.py:77
  154.4 30.3 %while.24 = (s32[]{:T(128)}, f32[8,64,128]{2,1,0:T(8,128)S(1)}, f32[2,256,8,64]{1,0,3,2:T(2,128)}, f32[2,256,8]{1,2,0:T(8,128)S(1)}, bf16[2,256,8,64]{1,3,2,0:T(...) while((s32[]{:T(128)}, f32[8,64,128]{2,1,0:T(8,128)S(1)}, ...), condition=%wide.region_3.4_spmd.clone, body=%wide.region_0.3_spmd.clone.sunk | while | flops 322801696 | bytes 6277456 | solution.py:98
  157.5 11.5 %dynamic_update_slice.6 = f32[2,256,8,64]{1,0,3,2:T(2,128)} dynamic-update-slice(f32[2,256,8,64]{1,0,3,2:T(2,128)} %get-tuple-element.276, f32[1,256,8,64]{1,0,3,2:T(1,128)S(1)} %copy.42, s32[]{:T(128)} %get-tuple-element.274, s32[]{:T(128)} %constant.46.clone.1..sunk, s32[]{:T(128)} %constant.46.clone.1..sunk, s32[]{:T(128)} %constant.46.clone.1..sunk) | dynamic-update-slice | bytes 1048580 | tf_op jit(solution)/shard_map/while/body/jit(dynamic_update_index_in_dim)/dynamic_update_slice | solution.py:98
  172.7 11.5 %dynamic_update_slice.6 = f32[2,256,8,64]{1,0,3,2:T(2,128)} dynamic-update-slice(f32[2,256,8,64]{1,0,3,2:T(2,128)} %get-tuple-element.276, f32[1,256,8,64]{1,0,3,2:T(1,128)S(1)} %copy.42, s32[]{:T(128)} %get-tuple-element.274, s32[]{:T(128)} %constant.46.clone.1..sunk, s32[]{:T(128)} %constant.46.clone.1..sunk, s32[]{:T(128)} %constant.46.clone.1..sunk) | dynamic-update-slice | bytes 1048580 | tf_op jit(solution)/shard_map/while/body/jit(dynamic_update_index_in_dim)/dynamic_update_slice | solution.py:98
  186.9 298.5 %while.23 = (s32[]{:T(128)}, f32[8,64,128]{2,1,0:T(8,128)S(1)}, pred[]{:T(512)}, f32[8]{0:T(128)S(1)}, f32[8,64,128]{2,1,0:T(8,128)S(1)}, /*index=5*/f32[8,64,128]{2,1,0:T(8,128)S(1)}, s32[]{:T(128)}) while((s32[]{:T(128)}, f32[8,64,128]{2,1,0:T(8,128)S(1)}, pred[]{:T(512)}, f32[8]{0:T(128)S(1)}, f32[8,64,128]{2,1,0:T(8,128)S(1)}, ...), condition=%wide.region_7.8_spmd, body=%wide.region_6.7_spmd.sunk | while | flops 196610 | bytes 2621590 | solution.py:109
  190.8 8.8 %collective-permute-done = f32[8,64,128]{2,1,0:T(8,128)S(1)} collective-permute-done((f32[8,64,128]{2,1,0:T(8,128)S(1)}, f32[8,64,128]{2,1,0:T(8,128)S(1)}, u32[]{:S(2)}, u32[]{:S(2)}) %collective-permute-start) | collective-permute-done | bytes 262176 | tf_op jit(solution)/shard_map/while/body/eval_jaxpr/ppermute | solution.py:21
  209.1 6.0 collective-permute-start
  279.5 6.0 collective-permute-start
  297.9 7.5 %collective-permute-start = (f32[8,64,128]{2,1,0:T(8,128)S(1)}, f32[8,64,128]{2,1,0:T(8,128)S(1)}, u32[]{:S(2)}, u32[]{:S(2)}) collective-permute-start(f32[8,64,128]{2,1,0:T(8,128)S(1)} %multiply_add_fusion.2), channel_id=1, source_target_pairs={{0,8},{8,16},{16,24},{24,32},{32,40},{40,48},{48,56},{56,64},{64,7... | collective-permute-start | bytes 786440 | tf_op jit(solution)/shard_map/while/body/eval_jaxpr/ppermute | solution.py:21
  353.7 5.6 collective-permute-start
  370.4 5.7 collective-permute-done
  403.2 6.3 %collective-permute-start = (f32[8,64,128]{2,1,0:T(8,128)S(1)}, f32[8,64,128]{2,1,0:T(8,128)S(1)}, u32[]{:S(2)}, u32[]{:S(2)}) collective-permute-start(f32[8,64,128]{2,1,0:T(8,128)S(1)} %multiply_add_fusion.2), channel_id=1, source_target_pairs={{0,8},{8,16},{16,24},{24,32},{32,40},{40,48},{48,56},{56,64},{64,7... | collective-permute-start | bytes 786440 | tf_op jit(solution)/shard_map/while/body/eval_jaxpr/ppermute | solution.py:21
  413.0 9.1 %collective-permute-start = (f32[8,64,128]{2,1,0:T(8,128)S(1)}, f32[8,64,128]{2,1,0:T(8,128)S(1)}, u32[]{:S(2)}, u32[]{:S(2)}) collective-permute-start(f32[8,64,128]{2,1,0:T(8,128)S(1)} %multiply_add_fusion.2), channel_id=1, source_target_pairs={{0,8},{8,16},{16,24},{24,32},{32,40},{40,48},{48,56},{56,64},{64,7... | collective-permute-start | bytes 786440 | tf_op jit(solution)/shard_map/while/body/eval_jaxpr/ppermute | solution.py:21
  442.5 6.2 collective-permute-start
  452.2 6.2 collective-permute-start
  462.3 6.2 collective-permute-start
  473.2 6.5 %collective-permute-start = (f32[8,64,128]{2,1,0:T(8,128)S(1)}, f32[8,64,128]{2,1,0:T(8,128)S(1)}, u32[]{:S(2)}, u32[]{:S(2)}) collective-permute-start(f32[8,64,128]{2,1,0:T(8,128)S(1)} %multiply_add_fusion.2), channel_id=1, source_target_pairs={{0,8},{8,16},{16,24},{24,32},{32,40},{40,48},{48,56},{56,64},{64,7... | collective-permute-start | bytes 786440 | tf_op jit(solution)/shard_map/while/body/eval_jaxpr/ppermute | solution.py:21
  493.0 45.8 %psum.7 = f32[512]{0:T(512)S(1)} all-reduce(f32[512]{0:T(512)S(1)} %get-tuple-element.160), channel_id=1, replica_groups=mesh['seq'=32,'head'=8] {'head'}, use_global_device_ids=true, to_apply=%region_9.10 | all-reduce | flops 512 | bytes 4096 | tf_op jit(solution)/shard_map/psum | solution.py:116
  538.8 7.8 %fusion.38 = f32[512,4096]{1,0:T(8,128)} fusion(bf16[512,4096]{1,0:T(8,128)(2,1)} %all-gather.5.cloned.1.call-done, f32[512,512]{1,0:T(8,128)S(1)} %get-tuple-element.161, f32[512]{0:T(512)S(1)} %copy-done.3, f32[512]{0:T(512)S(1)} %add_rsqrt_fusion), kind=kOutput, calls=%fused_computation.66 | convolution fusion | flops 2148270080 | bytes 13635584 | tf_op jit(solution)/shard_map/dot_general | solution.py:119
  546.6 76.3 %reduce-scatter.2.cloned.1.call-done = f32[512,512]{1,0:T(8,128)} async-done(((f32[512,4096]{1,0:T(8,128)}), f32[512,512]{1,0:T(8,128)}) %reduce-scatter.2.cloned.1.call-update) | async-done | bytes 1048592 | tf_op jit(solution)/shard_map/reduce_scatter | solution.py:122
  (209 shorter events, 256.6 us)
Async XLA Ops:
  6.5 123.1 %all-gather.3.cloned.1.call-start = ((), (), s32[]{:S(2)}) async-start(), calls=%async_computation.2 | async-start | bytes 8650752 | tf_op jit(solution)/shard_map/all_gather | solution.py:75
  9.7 71.0 %all-to-all-start = ((bf16[32,128,256]{2,1,0:T(8,128)(2,1)}), bf16[32,128,256]{2,1,0:T(8,128)(2,1)S(1)}, u32[]{:S(2)}, u32[]{:S(2)}) async-start(bf16[32,128,256]{2,1,0:T(8,128)(2,1)} %tile.2), calls=%async_computation | async-start | bytes 4194304 | tf_op jit(solution)/shard_map/all_to_all | solution.py:15
  21.7 517.0 %all-gather.5.cloned.1.call-start = ((), (), s32[]{:S(2)}) async-start(), calls=%async_computation.3 | async-start | bytes 4325376 | tf_op jit(solution)/shard_map/all_gather | solution.py:120
  22.5 600.4 %reduce-scatter.2.cloned.1.call-start = ((), (), s32[]{:S(2)}) async-start(), calls=%async_computation.4 | async-start | bytes 9437184 | tf_op jit(solution)/shard_map/reduce_scatter | solution.py:122
  187.0 12.6 %collective-permute-start = (f32[8,64,128]{2,1,0:T(8,128)S(1)}, f32[8,64,128]{2,1,0:T(8,128)S(1)}, u32[]{:S(2)}, u32[]{:S(2)}) collective-permute-start(f32[8,64,128]{2,1,0:T(8,128)S(1)} %multiply_add_fusion.2), channel_id=1, source_target_pairs={{0,8},{8,16},{16,24},{24,32},{32,40},{40,48},{48,56},{56,64},{64,7... | collective-permute-start | bytes 786440 | tf_op jit(solution)/shard_map/while/body/eval_jaxpr/ppermute | solution.py:21
  199.7 9.2 %collective-permute-start = (f32[8,64,128]{2,1,0:T(8,128)S(1)}, f32[8,64,128]{2,1,0:T(8,128)S(1)}, u32[]{:S(2)}, u32[]{:S(2)}) collective-permute-start(f32[8,64,128]{2,1,0:T(8,128)S(1)} %multiply_add_fusion.2), channel_id=1, source_target_pairs={{0,8},{8,16},{16,24},{24,32},{32,40},{40,48},{48,56},{56,64},{64,7... | collective-permute-start | bytes 786440 | tf_op jit(solution)/shard_map/while/body/eval_jaxpr/ppermute | solution.py:21
  209.1 10.3 %collective-permute-start = (f32[8,64,128]{2,1,0:T(8,128)S(1)}, f32[8,64,128]{2,1,0:T(8,128)S(1)}, u32[]{:S(2)}, u32[]{:S(2)}) collective-permute-start(f32[8,64,128]{2,1,0:T(8,128)S(1)} %multiply_add_fusion.2), channel_id=1, source_target_pairs={{0,8},{8,16},{16,24},{24,32},{32,40},{40,48},{48,56},{56,64},{64,7... | collective-permute-start | bytes 786440 | tf_op jit(solution)/shard_map/while/body/eval_jaxpr/ppermute | solution.py:21
  227.9 9.3 %collective-permute-start = (f32[8,64,128]{2,1,0:T(8,128)S(1)}, f32[8,64,128]{2,1,0:T(8,128)S(1)}, u32[]{:S(2)}, u32[]{:S(2)}) collective-permute-start(f32[8,64,128]{2,1,0:T(8,128)S(1)} %multiply_add_fusion.2), channel_id=1, source_target_pairs={{0,8},{8,16},{16,24},{24,32},{32,40},{40,48},{48,56},{56,64},{64,7... | collective-permute-start | bytes 786440 | tf_op jit(solution)/shard_map/while/body/eval_jaxpr/ppermute | solution.py:21
  237.4 9.4 %collective-permute-start = (f32[8,64,128]{2,1,0:T(8,128)S(1)}, f32[8,64,128]{2,1,0:T(8,128)S(1)}, u32[]{:S(2)}, u32[]{:S(2)}) collective-permute-start(f32[8,64,128]{2,1,0:T(8,128)S(1)} %multiply_add_fusion.2), channel_id=1, source_target_pairs={{0,8},{8,16},{16,24},{24,32},{32,40},{40,48},{48,56},{56,64},{64,7... | collective-permute-start | bytes 786440 | tf_op jit(solution)/shard_map/while/body/eval_jaxpr/ppermute | solution.py:21
  246.9 8.7 %collective-permute-start = (f32[8,64,128]{2,1,0:T(8,128)S(1)}, f32[8,64,128]{2,1,0:T(8,128)S(1)}, u32[]{:S(2)}, u32[]{:S(2)}) collective-permute-start(f32[8,64,128]{2,1,0:T(8,128)S(1)} %multiply_add_fusion.2), channel_id=1, source_target_pairs={{0,8},{8,16},{16,24},{24,32},{32,40},{40,48},{48,56},{56,64},{64,7... | collective-permute-start | bytes 786440 | tf_op jit(solution)/shard_map/while/body/eval_jaxpr/ppermute | solution.py:21
  279.5 9.3 %collective-permute-start = (f32[8,64,128]{2,1,0:T(8,128)S(1)}, f32[8,64,128]{2,1,0:T(8,128)S(1)}, u32[]{:S(2)}, u32[]{:S(2)}) collective-permute-start(f32[8,64,128]{2,1,0:T(8,128)S(1)} %multiply_add_fusion.2), channel_id=1, source_target_pairs={{0,8},{8,16},{16,24},{24,32},{32,40},{40,48},{48,56},{56,64},{64,7... | collective-permute-start | bytes 786440 | tf_op jit(solution)/shard_map/while/body/eval_jaxpr/ppermute | solution.py:21
  288.9 8.8 %collective-permute-start = (f32[8,64,128]{2,1,0:T(8,128)S(1)}, f32[8,64,128]{2,1,0:T(8,128)S(1)}, u32[]{:S(2)}, u32[]{:S(2)}) collective-permute-start(f32[8,64,128]{2,1,0:T(8,128)S(1)} %multiply_add_fusion.2), channel_id=1, source_target_pairs={{0,8},{8,16},{16,24},{24,32},{32,40},{40,48},{48,56},{56,64},{64,7... | collective-permute-start | bytes 786440 | tf_op jit(solution)/shard_map/while/body/eval_jaxpr/ppermute | solution.py:21
  297.9 10.7 %collective-permute-start = (f32[8,64,128]{2,1,0:T(8,128)S(1)}, f32[8,64,128]{2,1,0:T(8,128)S(1)}, u32[]{:S(2)}, u32[]{:S(2)}) collective-permute-start(f32[8,64,128]{2,1,0:T(8,128)S(1)} %multiply_add_fusion.2), channel_id=1, source_target_pairs={{0,8},{8,16},{16,24},{24,32},{32,40},{40,48},{48,56},{56,64},{64,7... | collective-permute-start | bytes 786440 | tf_op jit(solution)/shard_map/while/body/eval_jaxpr/ppermute | solution.py:21
  343.7 9.8 %collective-permute-start = (f32[8,64,128]{2,1,0:T(8,128)S(1)}, f32[8,64,128]{2,1,0:T(8,128)S(1)}, u32[]{:S(2)}, u32[]{:S(2)}) collective-permute-start(f32[8,64,128]{2,1,0:T(8,128)S(1)} %multiply_add_fusion.2), channel_id=1, source_target_pairs={{0,8},{8,16},{16,24},{24,32},{32,40},{40,48},{48,56},{56,64},{64,7... | collective-permute-start | bytes 786440 | tf_op jit(solution)/shard_map/while/body/eval_jaxpr/ppermute | solution.py:21
  353.7 11.3 %collective-permute-start = (f32[8,64,128]{2,1,0:T(8,128)S(1)}, f32[8,64,128]{2,1,0:T(8,128)S(1)}, u32[]{:S(2)}, u32[]{:S(2)}) collective-permute-start(f32[8,64,128]{2,1,0:T(8,128)S(1)} %multiply_add_fusion.2), channel_id=1, source_target_pairs={{0,8},{8,16},{16,24},{24,32},{32,40},{40,48},{48,56},{56,64},{64,7... | collective-permute-start | bytes 786440 | tf_op jit(solution)/shard_map/while/body/eval_jaxpr/ppermute | solution.py:21
  365.1 11.0 %collective-permute-start = (f32[8,64,128]{2,1,0:T(8,128)S(1)}, f32[8,64,128]{2,1,0:T(8,128)S(1)}, u32[]{:S(2)}, u32[]{:S(2)}) collective-permute-start(f32[8,64,128]{2,1,0:T(8,128)S(1)} %multiply_add_fusion.2), channel_id=1, source_target_pairs={{0,8},{8,16},{16,24},{24,32},{32,40},{40,48},{48,56},{56,64},{64,7... | collective-permute-start | bytes 786440 | tf_op jit(solution)/shard_map/while/body/eval_jaxpr/ppermute | solution.py:21
  376.3 9.9 %collective-permute-start = (f32[8,64,128]{2,1,0:T(8,128)S(1)}, f32[8,64,128]{2,1,0:T(8,128)S(1)}, u32[]{:S(2)}, u32[]{:S(2)}) collective-permute-start(f32[8,64,128]{2,1,0:T(8,128)S(1)} %multiply_add_fusion.2), channel_id=1, source_target_pairs={{0,8},{8,16},{16,24},{24,32},{32,40},{40,48},{48,56},{56,64},{64,7... | collective-permute-start | bytes 786440 | tf_op jit(solution)/shard_map/while/body/eval_jaxpr/ppermute | solution.py:21
  386.3 8.6 %collective-permute-start = (f32[8,64,128]{2,1,0:T(8,128)S(1)}, f32[8,64,128]{2,1,0:T(8,128)S(1)}, u32[]{:S(2)}, u32[]{:S(2)}) collective-permute-start(f32[8,64,128]{2,1,0:T(8,128)S(1)} %multiply_add_fusion.2), channel_id=1, source_target_pairs={{0,8},{8,16},{16,24},{24,32},{32,40},{40,48},{48,56},{56,64},{64,7... | collective-permute-start | bytes 786440 | tf_op jit(solution)/shard_map/while/body/eval_jaxpr/ppermute | solution.py:21
  403.2 9.6 %collective-permute-start = (f32[8,64,128]{2,1,0:T(8,128)S(1)}, f32[8,64,128]{2,1,0:T(8,128)S(1)}, u32[]{:S(2)}, u32[]{:S(2)}) collective-permute-start(f32[8,64,128]{2,1,0:T(8,128)S(1)} %multiply_add_fusion.2), channel_id=1, source_target_pairs={{0,8},{8,16},{16,24},{24,32},{32,40},{40,48},{48,56},{56,64},{64,7... | collective-permute-start | bytes 786440 | tf_op jit(solution)/shard_map/while/body/eval_jaxpr/ppermute | solution.py:21
  413.0 12.4 %collective-permute-start = (f32[8,64,128]{2,1,0:T(8,128)S(1)}, f32[8,64,128]{2,1,0:T(8,128)S(1)}, u32[]{:S(2)}, u32[]{:S(2)}) collective-permute-start(f32[8,64,128]{2,1,0:T(8,128)S(1)} %multiply_add_fusion.2), channel_id=1, source_target_pairs={{0,8},{8,16},{16,24},{24,32},{32,40},{40,48},{48,56},{56,64},{64,7... | collective-permute-start | bytes 786440 | tf_op jit(solution)/shard_map/while/body/eval_jaxpr/ppermute | solution.py:21
  442.5 9.5 %collective-permute-start = (f32[8,64,128]{2,1,0:T(8,128)S(1)}, f32[8,64,128]{2,1,0:T(8,128)S(1)}, u32[]{:S(2)}, u32[]{:S(2)}) collective-permute-start(f32[8,64,128]{2,1,0:T(8,128)S(1)} %multiply_add_fusion.2), channel_id=1, source_target_pairs={{0,8},{8,16},{16,24},{24,32},{32,40},{40,48},{48,56},{56,64},{64,7... | collective-permute-start | bytes 786440 | tf_op jit(solution)/shard_map/while/body/eval_jaxpr/ppermute | solution.py:21
  452.2 10.0 %collective-permute-start = (f32[8,64,128]{2,1,0:T(8,128)S(1)}, f32[8,64,128]{2,1,0:T(8,128)S(1)}, u32[]{:S(2)}, u32[]{:S(2)}) collective-permute-start(f32[8,64,128]{2,1,0:T(8,128)S(1)} %multiply_add_fusion.2), channel_id=1, source_target_pairs={{0,8},{8,16},{16,24},{24,32},{32,40},{40,48},{48,56},{56,64},{64,7... | collective-permute-start | bytes 786440 | tf_op jit(solution)/shard_map/while/body/eval_jaxpr/ppermute | solution.py:21
  462.3 10.7 %collective-permute-start = (f32[8,64,128]{2,1,0:T(8,128)S(1)}, f32[8,64,128]{2,1,0:T(8,128)S(1)}, u32[]{:S(2)}, u32[]{:S(2)}) collective-permute-start(f32[8,64,128]{2,1,0:T(8,128)S(1)} %multiply_add_fusion.2), channel_id=1, source_target_pairs={{0,8},{8,16},{16,24},{24,32},{32,40},{40,48},{48,56},{56,64},{64,7... | collective-permute-start | bytes 786440 | tf_op jit(solution)/shard_map/while/body/eval_jaxpr/ppermute | solution.py:21
  473.2 12.1 %collective-permute-start = (f32[8,64,128]{2,1,0:T(8,128)S(1)}, f32[8,64,128]{2,1,0:T(8,128)S(1)}, u32[]{:S(2)}, u32[]{:S(2)}) collective-permute-start(f32[8,64,128]{2,1,0:T(8,128)S(1)} %multiply_add_fusion.2), channel_id=1, source_target_pairs={{0,8},{8,16},{16,24},{24,32},{32,40},{40,48},{48,56},{56,64},{64,7... | collective-permute-start | bytes 786440 | tf_op jit(solution)/shard_map/while/body/eval_jaxpr/ppermute | solution.py:21
  (23 other events, 291.4 us)
Sparse Core Ops, SparseCore 0:
  9.9 119.6 all-gather.2
  132.1 85.2 all-gather.4
  546.7 76.1 reduce-scatter.1
